TPU v7x, 32 devices: a whole 2x2x4 slice. The times are simulated.
32 devices in a mesh: view: 4 (over x, core), samp: 8 (over z, y).
Axes of the slice: x: 2, y: 2, z: 4, core: 2. Of those that a mesh axis runs over, the one named last changes fastest.
Arguments:
- view_data: bfloat16 [8, 4096, 2048], P('view', 'samp'), may hold values from -10 to 10
- init_coeffs: float32 [8, 2048, 128], P('view'), may hold values from -0.125 to 0.125
Outputs:
- shared_scores: float32 [4096, 128], P('samp')
- final_coeffs: float32 [8, 2048, 128], P('view', 'samp')
All inputs are finite; a program needn't handle non-finite values.
Results may differ from a plain program's by a relative error of at most 0.005.
Values may be sent and summed in bfloat16 or wider, within the bound.
No kernel may reach another device: no remote copies, remote signals or barrier semaphores. Data moves between devices by JAX's collectives and lax.ppermute only.
A program may use at most 128 MiB of HBM per device.

v0:
```python
import jax
import jax.numpy as jnp
from jax import lax
from jax.sharding import PartitionSpec as P

OUTER = 2
INNER = 2
NS_ITERS = 12
HIGH = lax.Precision.HIGHEST
ridge_weight = 0.1
step_size = 0.5


def newton_inverse(gram):
    size_k = gram.shape[0]
    eye_mat = jnp.eye(size_k, dtype=jnp.float32)
    shrunk = gram + jnp.trace(gram) / size_k * eye_mat
    scale = jnp.sqrt(jnp.sum(shrunk * shrunk))
    approx = shrunk / scale
    inverse = eye_mat
    for turn in range(NS_ITERS):
        factor = 0.5 * (3.0 * eye_mat - jnp.dot(inverse, approx, precision=HIGH))
        approx = jnp.dot(approx, factor, precision=HIGH)
        inverse = jnp.dot(factor, inverse, precision=HIGH)
    return (inverse, scale)


def make_scores(view_data, coeffs_low, total):
    local_sum = jnp.zeros((view_data.shape[1], coeffs_low.shape[2]), jnp.float32)
    for member in range(view_data.shape[0]):
        local_sum = local_sum + jnp.dot(
            view_data[member], coeffs_low[member], preferred_element_type=jnp.float32
        )
    summed = lax.psum(local_sum, "view")
    gram = lax.psum(jnp.dot(summed.T, summed, precision=HIGH), "samp")
    inverse, scale = newton_inverse(gram)
    return jnp.dot(summed, inverse, precision=HIGH) * jnp.sqrt(total / scale)


def grad_term(samples, weights_low, scores):
    resid = (jnp.dot(samples, weights_low, preferred_element_type=jnp.float32) - scores).astype(
        jnp.bfloat16
    )
    return lax.dot_general(
        samples, resid, (((0,), (0,)), ((), ())), preferred_element_type=jnp.float32
    )


def body(view_data, init_coeffs):
    total = view_data.shape[1] * lax.axis_size("samp")
    row_count = init_coeffs.shape[1] // lax.axis_size("samp")
    row_start = lax.axis_index("samp") * row_count
    own_coeffs = lax.dynamic_slice_in_dim(init_coeffs, row_start, row_count, 1)
    coeffs_low = init_coeffs.astype(jnp.bfloat16)
    scores = make_scores(view_data, coeffs_low, total)
    for outer_step in range(OUTER):
        for inner_step in range(INNER):
            terms = jnp.stack(
                [
                    grad_term(view_data[member], coeffs_low[member], scores)
                    for member in range(view_data.shape[0])
                ]
            )
            summed_grad = lax.psum_scatter(terms, "samp", scatter_dimension=1, tiled=True)
            own_coeffs = own_coeffs - step_size * (summed_grad / total + ridge_weight * own_coeffs)
            coeffs_low = lax.all_gather(own_coeffs.astype(jnp.bfloat16), "samp", axis=1, tiled=True)
        scores = make_scores(view_data, coeffs_low, total)
    return (scores, own_coeffs)


def solution(mesh):
    in_specs = (P("view", "samp", None), P("view", None, None))
    out_specs = (P("samp", None), P("view", "samp", None))
    return jax.shard_map(body, mesh=mesh, in_specs=in_specs, out_specs=out_specs, check_vma=False)
```

profile of v0, /device:TPU:0, one launch (start us, length us, event | category | flops | bytes accessed | tf_op | source)
XLA Modules:
  0.0 856.1 jit_solution(11644975215844309981)
XLA Ops:
  7.2 1.9 convert_element_type.42
  9.1 2.3 fusion.12
  11.4 1.4 fusion.163
  12.9 35.1 %all-reduce.7.cloned.1.call-done = f32[512,128]{1,0:T(8,128)} async-done(((f32[512,128]{1,0:T(8,128)}), f32[512,128]{1,0:T(8,128)}) %all-reduce.7.cloned.1.call-update) | async-done | bytes 262160 | tf_op jit(solution)/shard_map/psum | solution.py:34
  48.0 2.2 fusion.165
  50.4 70.9 %all-reduce.9.cloned.1.call-done = f32[128,128]{1,0:T(8,128)} async-done(((f32[128,128]{1,0:T(8,128)}), f32[128,128]{1,0:T(8,128)}) %all-reduce.9.cloned.1.call-update) | async-done | bytes 65552 | tf_op jit(solution)/shard_map/psum | solution.py:35
  121.3 1.5 select_reduce_fusion.2
  123.4 1.5 multiply_reduce_fusion.2
  125.6 1.0 fusion.119
  126.8 1.1 fusion.152
  127.9 0.2 fusion.118
  129.8 0.2 fusion.115
  134.8 0.4 convolution_multiply_fusion.2
  135.1 2.3 convolution_bitcast_fusion.6
  137.6 0.5 convolution_bitcast_fusion.7
  138.0 1.5 pad_maximum_fusion
  139.6 1.0 constant_dynamic-slice_fusion
  140.7 67.8 %reduce-scatter.5.cloned.1.call-done = f32[2,256,128]{1,2,0:T(8,128)} async-done(((f32[2,2048,128]{1,2,0:T(8,128)}), f32[2,256,128]{1,2,0:T(8,128)}) %reduce-scatter.5.cloned.1.call-update) | async-done | bytes 262160 | tf_op jit(solution)/shard_map/reduce_scatter | solution.py:64
  208.5 1.7 fusion.144
  210.3 39.2 %all-gather.5.cloned.1.call-done = bf16[2,2048,128]{1,2,0:T(8,128)(2,1)} async-done(((bf16[2,256,128]{1,2,0:T(8,128)(2,1)}), bf16[2,2048,128]{1,2,0:T(8,128)(2,1)}) %all-gather.5.cloned.1.call-update) | async-done | bytes 1048592 | tf_op jit(solution)/shard_map/all_gather | solution.py:66
  249.5 4.0 convolution_bitcast_fusion.4
  253.4 4.0 convolution_bitcast_fusion.5
  257.4 1.5 pad_maximum_fusion.1
  259.0 68.0 %reduce-scatter.7.cloned.1.call-done = f32[2,256,128]{1,2,0:T(8,128)} async-done(((f32[2,2048,128]{1,2,0:T(8,128)}), f32[2,256,128]{1,2,0:T(8,128)}) %reduce-scatter.7.cloned.1.call-update) | async-done | bytes 262160 | tf_op jit(solution)/shard_map/reduce_scatter | solution.py:64
  327.0 1.7 fusion.162
  328.7 39.1 %all-gather.7.cloned.1.call-done = bf16[2,2048,128]{1,2,0:T(8,128)(2,1)} async-done(((bf16[2,256,128]{1,2,0:T(8,128)(2,1)}), bf16[2,2048,128]{1,2,0:T(8,128)(2,1)}) %all-gather.7.cloned.1.call-update) | async-done | bytes 1048592 | tf_op jit(solution)/shard_map/all_gather | solution.py:66
  367.9 2.7 fusion.55
  370.6 3.1 fusion.164
  373.7 0.2 all-reduce.13.cloned.1.call-start
  374.0 31.2 %all-reduce.11.cloned.1.call-done = f32[512,128]{0,1:T(8,128)} async-done(((f32[512,128]{0,1:T(8,128)}), f32[512,128]{0,1:T(8,128)}) %all-reduce.11.cloned.1.call-update) | async-done | bytes 262160 | tf_op jit(solution)/shard_map/psum | solution.py:34
  405.2 2.0 fusion.187
  407.3 71.1 %all-reduce.13.cloned.1.call-done = f32[128,128]{1,0:T(8,128)} async-done(((f32[128,128]{1,0:T(8,128)}), f32[128,128]{1,0:T(8,128)}) %all-reduce.13.cloned.1.call-update) | async-done | bytes 65552 | tf_op jit(solution)/shard_map/psum | solution.py:35
  478.4 1.5 select_reduce_fusion.1
  480.6 1.5 multiply_reduce_fusion.1
  482.8 1.0 fusion.107
  484.0 1.1 fusion.149
  485.0 0.2 fusion.106
  487.6 0.2 fusion.102
  490.8 0.2 fusion.97
  491.9 0.4 convolution_multiply_fusion.1
  492.3 2.3 convolution_bitcast_fusion.2
  494.7 0.4 convolution_bitcast_fusion.3
  495.2 1.5 pad_maximum_fusion.2
  496.7 69.1 %reduce-scatter.9.cloned.1.call-done = f32[2,256,128]{1,2,0:T(8,128)} async-done(((f32[2,2048,128]{1,2,0:T(8,128)}), f32[2,256,128]{1,2,0:T(8,128)}) %reduce-scatter.9.cloned.1.call-update) | async-done | bytes 262160 | tf_op jit(solution)/shard_map/reduce_scatter | solution.py:64
  565.8 1.7 fusion.145
  567.5 39.2 %all-gather.9.cloned.1.call-done = bf16[2,2048,128]{1,2,0:T(8,128)(2,1)} async-done(((bf16[2,256,128]{1,2,0:T(8,128)(2,1)}), bf16[2,2048,128]{1,2,0:T(8,128)(2,1)}) %all-gather.9.cloned.1.call-update) | async-done | bytes 1048592 | tf_op jit(solution)/shard_map/all_gather | solution.py:66
  606.7 3.6 convolution_bitcast_fusion
  610.3 3.6 convolution_bitcast_fusion.1
  613.9 1.5 pad_maximum_fusion.3
  615.5 68.0 %reduce-scatter.11.cloned.1.call-done = f32[2,256,128]{1,2,0:T(8,128)} async-done(((f32[2,2048,128]{1,2,0:T(8,128)}), f32[2,256,128]{1,2,0:T(8,128)}) %reduce-scatter.11.cloned.1.call-update) | async-done | bytes 262160 | tf_op jit(solution)/shard_map/reduce_scatter | solution.py:64
  683.5 1.7 fusion.161
  685.3 39.1 %all-gather.11.cloned.1.call-done = bf16[2,2048,128]{1,2,0:T(8,128)(2,1)} async-done(((bf16[2,256,128]{1,2,0:T(8,128)(2,1)}), bf16[2,2048,128]{1,2,0:T(8,128)(2,1)}) %all-gather.11.cloned.1.call-update) | async-done | bytes 1048592 | tf_op jit(solution)/shard_map/all_gather | solution.py:66
  724.4 2.7 fusion
  727.1 3.1 fusion.46
  730.3 0.3 all-reduce.17.cloned.1.call-start
  730.5 31.2 %all-reduce.15.cloned.1.call-done = f32[512,128]{0,1:T(8,128)} async-done(((f32[512,128]{0,1:T(8,128)}), f32[512,128]{0,1:T(8,128)}) %all-reduce.15.cloned.1.call-update) | async-done | bytes 262160 | tf_op jit(solution)/shard_map/psum | solution.py:34
  761.7 2.0 fusion.209
  763.8 0.8 copy.6
  764.6 70.2 %all-reduce.17.cloned.1.call-done = f32[128,128]{1,0:T(8,128)} async-done(((f32[128,128]{1,0:T(8,128)}), f32[128,128]{1,0:T(8,128)}) %all-reduce.17.cloned.1.call-update) | async-done | bytes 65552 | tf_op jit(solution)/shard_map/psum | solution.py:35
  834.8 1.5 select_reduce_fusion
  837.0 1.5 multiply_reduce_fusion
  839.2 1.0 fusion.95
  840.4 1.1 fusion.146
  848.3 1.3 convolution_multiply_fusion
  (141 shorter events, 20.3 us)
Async XLA Ops:
  7.2 40.9 %all-reduce.7.cloned.1.call-start = ((), (), s32[]{:S(2)}) async-start(), calls=%async_computation.4 | async-start | bytes 524288 | tf_op jit(solution)/shard_map/psum | solution.py:34
  7.2 4.2 copy-start
  12.9 108.4 %all-reduce.9.cloned.1.call-start = ((), (), s32[]{:S(2)}) async-start(), calls=%async_computation.5 | async-start | bytes 131072 | tf_op jit(solution)/shard_map/psum | solution.py:35
  50.3 158.2 %reduce-scatter.5.cloned.1.call-start = ((), (), s32[]{:S(2)}) async-start(), calls=%async_computation.6 | async-start | bytes 2359296 | tf_op jit(solution)/shard_map/reduce_scatter | solution.py:64
  130.2 4.5 copy-start.4
  134.7 2.8 copy-start.1
  139.6 109.9 %all-gather.5.cloned.1.call-start = ((), (), s32[]{:S(2)}) async-start(), calls=%async_computation.7 | async-start | bytes 1179648 | tf_op jit(solution)/shard_map/all_gather | solution.py:66
  210.2 116.8 %reduce-scatter.7.cloned.1.call-start = ((), (), s32[]{:S(2)}) async-start(), calls=%async_computation.8 | async-start | bytes 2359296 | tf_op jit(solution)/shard_map/reduce_scatter | solution.py:64
  258.9 68.1 %copy-start.6 = (f32[2,256,128]{1,2,0:T(8,128)S(1)}, f32[2,256,128]{1,2,0:T(8,128)}, u32[]{:S(2)}) copy-start(f32[2,256,128]{1,2,0:T(8,128)} %reduce-scatter.5.cloned.1.call-done) | copy-start | bytes 786436
  258.9 109.0 %all-gather.7.cloned.1.call-start = ((), (), s32[]{:S(2)}) async-start(), calls=%async_computation.9 | async-start | bytes 1179648 | tf_op jit(solution)/shard_map/all_gather | solution.py:66
  328.7 76.5 %all-reduce.11.cloned.1.call-start = ((), (), s32[]{:S(2)}) async-start(), calls=%async_computation.10 | async-start | bytes 524288 | tf_op jit(solution)/shard_map/psum | solution.py:34
  367.9 2.7 copy-start.8
  373.7 104.7 %all-reduce.13.cloned.1.call-start = ((), (), s32[]{:S(2)}) async-start(), calls=%async_computation.11 | async-start | bytes 131072 | tf_op jit(solution)/shard_map/psum | solution.py:35
  407.3 158.5 %reduce-scatter.9.cloned.1.call-start = ((), (), s32[]{:S(2)}) async-start(), calls=%async_computation.12 | async-start | bytes 2359296 | tf_op jit(solution)/shard_map/reduce_scatter | solution.py:64
  487.4 4.5 copy-start.5
  491.9 2.8 copy-start.2
  496.7 110.0 %all-gather.9.cloned.1.call-start = ((), (), s32[]{:S(2)}) async-start(), calls=%async_computation.13 | async-start | bytes 1179648 | tf_op jit(solution)/shard_map/all_gather | solution.py:66
  567.5 116.0 %reduce-scatter.11.cloned.1.call-start = ((), (), s32[]{:S(2)}) async-start(), calls=%async_computation.14 | async-start | bytes 2359296 | tf_op jit(solution)/shard_map/reduce_scatter | solution.py:64
  615.4 68.1 %copy-start.7 = (f32[2,256,128]{1,2,0:T(8,128)S(1)}, f32[2,256,128]{1,2,0:T(8,128)}, u32[]{:S(2)}) copy-start(f32[2,256,128]{1,2,0:T(8,128)} %reduce-scatter.9.cloned.1.call-done) | copy-start | bytes 786436
  615.4 109.0 %all-gather.11.cloned.1.call-start = ((), (), s32[]{:S(2)}) async-start(), calls=%async_computation.15 | async-start | bytes 1179648 | tf_op jit(solution)/shard_map/all_gather | solution.py:66
  685.2 76.5 %all-reduce.15.cloned.1.call-start = ((), (), s32[]{:S(2)}) async-start(), calls=%async_computation.16 | async-start | bytes 524288 | tf_op jit(solution)/shard_map/psum | solution.py:34
  724.4 2.7 copy-start.9
  730.3 104.6 %all-reduce.17.cloned.1.call-start = ((), (), s32[]{:S(2)}) async-start(), calls=%async_computation.17 | async-start | bytes 131072 | tf_op jit(solution)/shard_map/psum | solution.py:35
  843.8 4.5 copy-start.3
Sparse Core Ops, SparseCore 0:
  13.0 35.0 all-reduce.6
  52.0 69.2 all-reduce.8
  139.7 68.8 reduce-scatter.4
  211.0 38.3 all-gather.4
  259.0 67.8 reduce-scatter.6
  329.4 38.4 all-gather.6
  373.9 31.2 all-reduce.10
  409.2 69.2 all-reduce.12
  496.8 68.9 reduce-scatter.8
  568.2 38.3 all-gather.8
  615.6 67.9 reduce-scatter.10
  686.0 38.3 all-gather.10
  730.4 31.2 all-reduce.14
  765.6 69.2 all-reduce.16
where the time goes:
time: 857 us; the launch traced here: 856 us
  waiting for transfers between devices  740 us (86%)
  matrix products  70.7 us (8%)
  other arithmetic  23.3 us (3%)
  between operations  19.3 us (2%)
    reduce_scatter x4, waiting for transfers between devices, body(): lax.psum_scatter(terms, 'samp', scatter_dimension=1, tiled=True)  273 us
    psum x3, waiting for transfers between devices, make_scores(): gram = lax.psum(jnp.dot(summed.T, summed, precision=HIGH), 'samp')  212 us
    all_gather x4, waiting for transfers between devices, body(): lax.all_gather(own_coeffs.astype(jnp.bfloat16), 'samp', axis=1, tiled=True)  157 us
    psum x3, waiting for transfers between devices, make_scores(): summed = lax.psum(local_sum, 'view')  97.5 us
    dot_general x8, matrix products, grad_term(): lax.dot_general(samples, resid, (((0,), (0,)), ((), ())), preferred_eleme...  20.6 us
  transfers between devices with their start and end apart: 14, of which 14 were waited for; matrix products, arithmetic and copies ran while one was open for 0% of the time, Pallas kernels for 0%

commit v1 on v0

--- a/solution.py
+++ b/solution.py
@@ -63,7 +63,17 @@
             )
             summed_grad = lax.psum_scatter(terms, "samp", scatter_dimension=1, tiled=True)
             own_coeffs = own_coeffs - step_size * (summed_grad / total + ridge_weight * own_coeffs)
-            coeffs_low = lax.all_gather(own_coeffs.astype(jnp.bfloat16), "samp", axis=1, tiled=True)
+
+            def clear_strings(panel):
+                arrivals = []
+                for _ in range(lax.axis_size("samp")):
+                    arrivals.append(panel)
+                f_now = lax.all_to_all(
+                    jnp.stack(arrivals), axis_name="samp", split_axis=0, concat_axis=0
+                )
+                return jnp.concatenate(f_now, axis=1)
+
+            coeffs_low = clear_strings(own_coeffs.astype(jnp.bfloat16))
         scores = make_scores(view_data, coeffs_low, total)
     return (scores, own_coeffs)
 

time: 857 us -> 802 us (0.936)
  waiting for transfers between devices: 740 us -> 582 us
  blocking collectives: 0 us -> 111 us
    all_gather x4 -> x0, waiting for transfers between devices: 157 us -> none  [body(): lax.all_gather(own_coeffs.astype(jnp.bfloat16), 'samp', axis=1, tiled=True)]
    all_to_all x0 -> x4, blocking collectives: none -> 111 us  [clear_strings(): lax.all_to_all(jnp.stack(arrivals), axis_name='samp', split_axis=0, conca...]
  transfers between devices with their start and end apart: 14 -> 10, of which waited for: 14 -> 10; matrix products, arithmetic and copies ran while one was open for 0% -> 0% of each run, Pallas kernels for 0% -> 0%
where the time goes in v1:
time: 802 us; the launch traced here: 801 us
  waiting for transfers between devices  582 us (73%)
  blocking collectives  111 us (14%)
  matrix products  63.1 us (8%)
  other arithmetic  20.7 us (3%)
  between operations  19.6 us (2%)
    reduce_scatter x4, waiting for transfers between devices, body(): lax.psum_scatter(terms, 'samp', scatter_dimension=1, tiled=True)  273 us
    psum x3, waiting for transfers between devices, make_scores(): gram = lax.psum(jnp.dot(summed.T, summed, precision=HIGH), 'samp')  212 us
    all_to_all x4, blocking collectives, clear_strings(): lax.all_to_all(jnp.stack(arrivals), axis_name='samp', split_axis=0, conca...  111 us
    psum x3, waiting for transfers between devices, make_scores(): summed = lax.psum(local_sum, 'view')  97.6 us
    dot_general x8, matrix products, grad_term(): lax.dot_general(samples, resid, (((0,), (0,)), ((), ())), preferred_eleme...  19.9 us
  transfers between devices with their start and end apart: 10, of which 10 were waited for; matrix products, arithmetic and copies ran while one was open for 0% of the time, Pallas kernels for 0%

profile of v1, /device:TPU:0, one launch (start us, length us, event | category | flops | bytes accessed | tf_op | source)
XLA Modules:
  0.0 801.4 jit_solution(9886404011825219546)
XLA Ops:
  7.2 1.9 convert_element_type.42
  9.1 2.3 fusion.12
  11.4 1.4 fusion.167
  12.9 35.1 %all-reduce.7.cloned.1.call-done = f32[512,128]{1,0:T(8,128)} async-done(((f32[512,128]{1,0:T(8,128)}), f32[512,128]{1,0:T(8,128)}) %all-reduce.7.cloned.1.call-update) | async-done | bytes 262160 | tf_op jit(solution)/shard_map/psum | solution.py:34
  48.0 2.2 fusion.169
  50.4 70.9 %all-reduce.9.cloned.1.call-done = f32[128,128]{1,0:T(8,128)} async-done(((f32[128,128]{1,0:T(8,128)}), f32[128,128]{1,0:T(8,128)}) %all-reduce.9.cloned.1.call-update) | async-done | bytes 65552 | tf_op jit(solution)/shard_map/psum | solution.py:35
  121.3 1.5 select_reduce_fusion.2
  123.4 1.5 multiply_reduce_fusion.2
  125.6 1.0 fusion.119
  126.8 1.1 fusion.152
  127.9 0.2 fusion.118
  129.8 0.2 fusion.115
  134.8 0.4 convolution_multiply_fusion.2
  135.1 2.3 convolution_bitcast_fusion.6
  137.6 0.5 convolution_bitcast_fusion.7
  138.0 1.5 pad_maximum_fusion
  139.6 1.0 constant_dynamic-slice_fusion
  140.7 67.8 %reduce-scatter.5.cloned.1.call-done = f32[2,256,128]{1,2,0:T(8,128)} async-done(((f32[2,2048,128]{1,2,0:T(8,128)}), f32[2,256,128]{1,2,0:T(8,128)}) %reduce-scatter.5.cloned.1.call-update) | async-done | bytes 262160 | tf_op jit(solution)/shard_map/reduce_scatter | solution.py:64
  208.5 1.0 fusion.144
  209.9 27.6 %all_to_all.20 = bf16[8,2,256,128]{3,2,1,0:T(8,128)(2,1)S(1)} all-to-all(bf16[8,2,256,128]{3,2,1,0:T(8,128)(2,1)S(1)} %stack.35), channel_id=1, replica_groups=mesh['view'=4,'samp'=8] {'samp'}, dimensions={0} | all-to-all | bytes 2097152 | tf_op jit(solution)/shard_map/all_to_all | solution.py:71
  237.5 3.8 convolution_bitcast_fusion.4
  241.4 3.8 convolution_bitcast_fusion.5
  245.2 1.5 pad_maximum_fusion.1
  246.7 67.9 %reduce-scatter.7.cloned.1.call-done = f32[2,256,128]{1,2,0:T(8,128)} async-done(((f32[2,2048,128]{1,2,0:T(8,128)}), f32[2,256,128]{1,2,0:T(8,128)}) %reduce-scatter.7.cloned.1.call-update) | async-done | bytes 262160 | tf_op jit(solution)/shard_map/reduce_scatter | solution.py:64
  314.7 1.0 fusion.162
  316.1 27.9 %all_to_all.21 = bf16[8,2,256,128]{3,2,1,0:T(8,128)(2,1)S(1)} all-to-all(bf16[8,2,256,128]{3,2,1,0:T(8,128)(2,1)S(1)} %stack.39), channel_id=1, replica_groups=mesh['view'=4,'samp'=8] {'samp'}, dimensions={0} | all-to-all | bytes 2097152 | tf_op jit(solution)/shard_map/all_to_all | solution.py:71
  344.0 0.8 fusion.55
  344.9 1.5 fusion.168
  346.5 31.4 %all-reduce.11.cloned.1.call-done = f32[512,128]{0,1:T(8,128)} async-done(((f32[512,128]{0,1:T(8,128)}), f32[512,128]{0,1:T(8,128)}) %all-reduce.11.cloned.1.call-update) | async-done | bytes 262160 | tf_op jit(solution)/shard_map/psum | solution.py:34
  377.8 2.0 fusion.191
  380.0 71.0 %all-reduce.13.cloned.1.call-done = f32[128,128]{1,0:T(8,128)} async-done(((f32[128,128]{1,0:T(8,128)}), f32[128,128]{1,0:T(8,128)}) %all-reduce.13.cloned.1.call-update) | async-done | bytes 65552 | tf_op jit(solution)/shard_map/psum | solution.py:35
  451.0 1.5 select_reduce_fusion.1
  453.1 1.5 multiply_reduce_fusion.1
  455.3 1.0 fusion.107
  456.5 1.1 fusion.149
  459.5 0.2 fusion.103
  460.7 0.2 fusion.101
  463.3 0.2 fusion.97
  464.4 0.4 convolution_multiply_fusion.1
  464.8 2.3 convolution_bitcast_fusion.2
  467.2 0.4 convolution_bitcast_fusion.3
  467.7 1.5 pad_maximum_fusion.2
  469.2 68.9 %reduce-scatter.9.cloned.1.call-done = f32[2,256,128]{1,2,0:T(8,128)} async-done(((f32[2,2048,128]{1,2,0:T(8,128)}), f32[2,256,128]{1,2,0:T(8,128)}) %reduce-scatter.9.cloned.1.call-update) | async-done | bytes 262160 | tf_op jit(solution)/shard_map/reduce_scatter | solution.py:64
  538.1 1.0 fusion.145
  539.5 27.6 %all_to_all.22 = bf16[8,2,256,128]{3,2,1,0:T(8,128)(2,1)S(1)} all-to-all(bf16[8,2,256,128]{3,2,1,0:T(8,128)(2,1)S(1)} %stack.43), channel_id=1, replica_groups=mesh['view'=4,'samp'=8] {'samp'}, dimensions={0} | all-to-all | bytes 2097152 | tf_op jit(solution)/shard_map/all_to_all | solution.py:71
  567.2 3.4 convolution_bitcast_fusion
  570.6 3.4 convolution_bitcast_fusion.1
  574.1 1.5 pad_maximum_fusion.3
  575.6 67.9 %reduce-scatter.11.cloned.1.call-done = f32[2,256,128]{1,2,0:T(8,128)} async-done(((f32[2,2048,128]{1,2,0:T(8,128)}), f32[2,256,128]{1,2,0:T(8,128)}) %reduce-scatter.11.cloned.1.call-update) | async-done | bytes 262160 | tf_op jit(solution)/shard_map/reduce_scatter | solution.py:64
  643.6 1.0 fusion.161
  645.0 27.9 %all_to_all.23 = bf16[8,2,256,128]{3,2,1,0:T(8,128)(2,1)S(1)} all-to-all(bf16[8,2,256,128]{3,2,1,0:T(8,128)(2,1)S(1)} %stack.47), channel_id=1, replica_groups=mesh['view'=4,'samp'=8] {'samp'}, dimensions={0} | all-to-all | bytes 2097152 | tf_op jit(solution)/shard_map/all_to_all | solution.py:71
  672.9 0.8 fusion
  673.7 1.5 fusion.46
  675.3 0.3 all-reduce.17.cloned.1.call-start
  675.6 31.1 %all-reduce.15.cloned.1.call-done = f32[512,128]{0,1:T(8,128)} async-done(((f32[512,128]{0,1:T(8,128)}), f32[512,128]{0,1:T(8,128)}) %all-reduce.15.cloned.1.call-update) | async-done | bytes 262160 | tf_op jit(solution)/shard_map/psum | solution.py:34
  706.7 2.0 fusion.213
  708.8 0.8 copy.10
  709.6 70.2 %all-reduce.17.cloned.1.call-done = f32[128,128]{1,0:T(8,128)} async-done(((f32[128,128]{1,0:T(8,128)}), f32[128,128]{1,0:T(8,128)}) %all-reduce.17.cloned.1.call-update) | async-done | bytes 65552 | tf_op jit(solution)/shard_map/psum | solution.py:35
  779.8 1.5 select_reduce_fusion
  781.9 1.5 multiply_reduce_fusion
  784.1 1.0 fusion.95
  785.3 1.1 fusion.146
  787.7 0.2 fusion.92
  793.2 1.3 convolution_multiply_fusion
  (145 shorter events, 21.5 us)
Async XLA Ops:
  7.2 40.9 %all-reduce.7.cloned.1.call-start = ((), (), s32[]{:S(2)}) async-start(), calls=%async_computation.8 | async-start | bytes 524288 | tf_op jit(solution)/shard_map/psum | solution.py:34
  7.2 4.2 copy-start
  12.9 108.4 %all-reduce.9.cloned.1.call-start = ((), (), s32[]{:S(2)}) async-start(), calls=%async_computation.9 | async-start | bytes 131072 | tf_op jit(solution)/shard_map/psum | solution.py:35
  50.3 158.2 %reduce-scatter.5.cloned.1.call-start = ((), (), s32[]{:S(2)}) async-start(), calls=%async_computation.10 | async-start | bytes 2359296 | tf_op jit(solution)/shard_map/reduce_scatter | solution.py:64
  130.2 4.5 copy-start.6
  134.7 2.8 copy-start.1
  139.6 175.1 %reduce-scatter.7.cloned.1.call-start = ((), (), s32[]{:S(2)}) async-start(), calls=%async_computation.11 | async-start | bytes 2359296 | tf_op jit(solution)/shard_map/reduce_scatter | solution.py:64
  246.7 68.0 %copy-start.8 = (f32[2,256,128]{1,2,0:T(8,128)S(1)}, f32[2,256,128]{1,2,0:T(8,128)}, u32[]{:S(2)}) copy-start(f32[2,256,128]{1,2,0:T(8,128)} %reduce-scatter.5.cloned.1.call-done) | copy-start | bytes 786436
  246.7 131.1 %all-reduce.11.cloned.1.call-start = ((), (), s32[]{:S(2)}) async-start(), calls=%async_computation.12 | async-start | bytes 524288 | tf_op jit(solution)/shard_map/psum | solution.py:34
  316.1 28.0 %copy-start.2 = (bf16[2,512,2048]{2,1,0:T(8,128)(2,1)S(1)}, bf16[2,512,2048]{2,1,0:T(8,128)(2,1)}, u32[]{:S(2)}) copy-start(bf16[2,512,2048]{2,1,0:T(8,128)(2,1)} %param.2) | copy-start | bytes 12582916
  346.4 104.5 %all-reduce.13.cloned.1.call-start = ((), (), s32[]{:S(2)}) async-start(), calls=%async_computation.13 | async-start | bytes 131072 | tf_op jit(solution)/shard_map/psum | solution.py:35
  379.9 158.2 %reduce-scatter.9.cloned.1.call-start = ((), (), s32[]{:S(2)}) async-start(), calls=%async_computation.14 | async-start | bytes 2359296 | tf_op jit(solution)/shard_map/reduce_scatter | solution.py:64
  459.9 4.5 copy-start.7
  464.4 2.8 copy-start.3
  469.2 174.4 %reduce-scatter.11.cloned.1.call-start = ((), (), s32[]{:S(2)}) async-start(), calls=%async_computation.15 | async-start | bytes 2359296 | tf_op jit(solution)/shard_map/reduce_scatter | solution.py:64
  575.5 68.0 %copy-start.9 = (f32[2,256,128]{1,2,0:T(8,128)S(1)}, f32[2,256,128]{1,2,0:T(8,128)}, u32[]{:S(2)}) copy-start(f32[2,256,128]{1,2,0:T(8,128)} %reduce-scatter.9.cloned.1.call-done) | copy-start | bytes 786436
  575.6 131.1 %all-reduce.15.cloned.1.call-start = ((), (), s32[]{:S(2)}) async-start(), calls=%async_computation.16 | async-start | bytes 524288 | tf_op jit(solution)/shard_map/psum | solution.py:34
  644.9 28.0 %copy-start.4 = (bf16[2,512,2048]{2,1,0:T(8,128)(2,1)S(1)}, bf16[2,512,2048]{2,1,0:T(8,128)(2,1)}, u32[]{:S(2)}) copy-start(bf16[2,512,2048]{2,1,0:T(8,128)(2,1)} %param.2) | copy-start | bytes 12582916
  675.3 104.5 %all-reduce.17.cloned.1.call-start = ((), (), s32[]{:S(2)}) async-start(), calls=%async_computation.17 | async-start | bytes 131072 | tf_op jit(solution)/shard_map/psum | solution.py:35
  788.7 4.5 copy-start.5
Sparse Core Ops, SparseCore 0:
  13.0 35.0 all-reduce.6
  52.0 69.2 all-reduce.8
  139.7 68.8 reduce-scatter.4
  246.8 67.8 reduce-scatter.6
  346.6 31.2 all-reduce.10
  381.7 69.2 all-reduce.12
  469.3 68.7 reduce-scatter.8
  575.7 67.8 reduce-scatter.10
  675.4 31.2 all-reduce.14
  710.5 69.2 all-reduce.16
